TPU v7x, 128 devices: a whole 4x4x4 slice. The times are simulated.
128 devices in a mesh: row: 8 (over z, y_lo), col: 16 (over x, y_hi, core).
Axes of the slice: x: 4, y: 4 (y_hi: 2, y_lo: 2; y = y_hi * 2 + y_lo), z: 4, core: 2. Of those that a mesh axis runs over, the one named last changes fastest.
Arguments:
- integrals: bfloat16 [10240, 10240], P('row', 'col'), may hold values from -6 to 6
- amplitudes: bfloat16 [10240, 8192], P('row', 'col'), may hold values from -0.0625 to 0.0625
- int_shape: int32 [40, 40], P('row'), may hold values 0 or 1
- amp_shape: int32 [40, 32], P(None, 'col'), may hold values 0 or 1
Outputs:
- ladder: bfloat16 [10240, 8192], P('row', 'col')
All inputs are finite; a program needn't handle non-finite values. No bound on the sum of `int_shape` or of `amp_shape` on one device may be relied on, other than what follows from the above.
Results may differ from a plain program's by a relative error of at most 0.001.
Values may be sent and summed in bfloat16 or wider, within the bound.
No kernel may reach another device: no remote copies, remote signals or barrier semaphores. Data moves between devices by JAX's collectives and lax.ppermute only.
A program may use at most 192 MiB of HBM per device.

v0:
```python
import jax
import jax.numpy as jnp
from jax import lax
from jax.sharding import PartitionSpec as P

TILE = 256


def expand_shape(shape_mask):
    return jnp.repeat(jnp.repeat(shape_mask, TILE, axis=0), TILE, axis=1).astype(jnp.bfloat16)


def per_device(integrals, amplitudes, int_shape, amp_shape):
    int_mask = expand_shape(int_shape)
    amp_mask = expand_shape(amp_shape)
    whole_amp = lax.all_gather(amplitudes, "row", axis=0, tiled=True) * amp_mask
    left = lax.all_gather(integrals, "col", axis=1, tiled=True) * int_mask
    total = jnp.dot(left, whole_amp, preferred_element_type=jnp.float32)
    return total.astype(jnp.bfloat16)


def solution(mesh):
    in_specs = (P("row", "col"), P("row", "col"), P("row", None), P(None, "col"))
    out_specs = P("row", "col")
    return jax.shard_map(
        per_device, mesh=mesh, in_specs=in_specs, out_specs=out_specs, check_vma=False
    )
```

profile of v0, /device:TPU:1, one launch (start us, length us, event | category | flops | bytes accessed | tf_op | source)
XLA Modules:
  0.0 410.5 jit_solution(6335129066689984502)
XLA Ops:
  6.5 0.0 all-gather.5.cloned.1.call-start
  6.5 0.7 all-gather.5.cloned.1.call-update
  7.3 0.0 all-gather.3.cloned.1.call-start
  7.3 0.7 all-gather.3.cloned.1.call-update
  8.0 0.7 convert_element_type.25
  8.7 12.1 %broadcast_in_dim.13 = bf16[1280,40,256]{2,1,0:T(8,128)(2,1)} broadcast(bf16[1280,40]{1,0:T(8,128)(2,1)S(1)} %bitcast.11), dimensions={0,1} | broadcast | bytes 26316800 | tf_op jit(solution)/shard_map/broadcast_in_dim | solution.py:10
  20.8 0.0 copy-start
  20.8 23.5 %copy.6 = bf16[160,8,40,256]{3,1,2,0:T(8,128)(2,1)} copy(bf16[160,8,40,256]{3,2,1,0:T(8,128)(2,1)} %bitcast.6) | data formatting | bytes 52428800
  44.3 0.0 copy-done
  44.3 0.1 copy.5
  44.4 0.3 broadcast_in_dim.14
  44.8 12.5 %broadcast_in_dim.15 = bf16[10240,2,256]{2,1,0:T(2,128)(2,1)S(1)} broadcast(bf16[10240,2]{1,0:T(8,128)(2,1)S(1)} %bitcast.10), dimensions={0,1} | broadcast | bytes 10526720 | tf_op jit(solution)/shard_map/broadcast_in_dim | solution.py:10
  57.3 7.3 %copy.7 = bf16[1280,8,2,256]{3,1,2,0:T(8,128)(2,1)} copy(bf16[1280,8,2,256]{3,2,1,0:T(2,128)(2,1)S(1)} %bitcast.7) | data formatting | bytes 20971520
  64.6 155.3 %all-gather.5.cloned.1.call-done = bf16[10240,512]{1,0:T(8,128)(2,1)} async-done(((bf16[1280,512]{1,0:T(8,128)(2,1)}), bf16[10240,512]{1,0:T(8,128)(2,1)}) %all-gather.5.cloned.1.call-update) | async-done | bytes 10485776 | tf_op jit(solution)/shard_map/all_gather | solution.py:16
  219.9 156.8 %all-gather.3.cloned.1.call-done = bf16[1280,10240]{1,0:T(8,128)(2,1)} async-done(((bf16[1280,640]{1,0:T(8,128)(2,1)}), bf16[1280,10240]{1,0:T(8,128)(2,1)}) %all-gather.3.cloned.1.call-update) | async-done | bytes 26214416 | tf_op jit(solution)/shard_map/all_gather | solution.py:17
  376.7 27.0 %fusion.3 = bf16[1280,512]{1,0:T(8,128)(2,1)} fusion(bf16[10240,512]{1,0:T(8,128)(2,1)} %all-gather.5.cloned.1.call-done, bf16[10240,512]{1,0:T(8,128)(2,1)} %bitcast.9, bf16[1280,10240]{1,0:T(8,128)(2,1)} %all-gather.3.cloned.1.call-done, bf16[1280,10240]{1,0:T(8,128)(2,1)} %bitcast.8), kind=kOutput, calls=%fused_computation.3 | convolution fusion | flops 13440778240 | bytes 74711040 | tf_op jit(solution)/shard_map/dot_general | solution.py:18
  (2 shorter events, 0.1 us)
Async XLA Ops:
  6.5 213.4 %all-gather.5.cloned.1.call-start = ((), (), s32[]{:S(2)}) async-start(), calls=%async_computation.1 | async-start | bytes 11796480 | tf_op jit(solution)/shard_map/all_gather | solution.py:16
  7.3 369.4 %all-gather.3.cloned.1.call-start = ((), (), s32[]{:S(2)}) async-start(), calls=%async_computation | async-start | bytes 27852800 | tf_op jit(solution)/shard_map/all_gather | solution.py:17
  20.8 23.5 %copy-start = (s32[40,2]{0,1:T(2,128)S(1)}, s32[40,2]{0,1:T(2,128)}, u32[]{:S(2)}) copy-start(s32[40,2]{0,1:T(2,128)} %param.7) | copy-start | bytes 964
Sparse Core Ops, SparseCore 0:
  9.0 210.8 all-gather.4
  222.4 154.2 all-gather.2
where the time goes:
time: 411 us
  waiting for transfers between devices  314 us (76%)
  local copies, waits for them, and re-layouts  55.8 us (14%)
  matrix products  27 us (7%)
  between operations  13.4 us (3%)
    all_gather x1, waiting for transfers between devices, per_device(): left = lax.all_gather(integrals, 'col', axis=1, tiled=True) * int_mask  157 us
    all_gather x1, waiting for transfers between devices, per_device(): whole_amp = lax.all_gather(amplitudes, 'row', axis=0, tiled=True) * amp_mask  155 us
    unnamed x4, local copies, waits for them, and re-layouts  30.7 us
    dot_general x1, matrix products, per_device(): total = jnp.dot(left, whole_amp, preferred_element_type=jnp.float32)  27 us
    broadcast_in_dim x2, local copies, waits for them, and re-layouts, expand_shape(): jnp.repeat(jnp.repeat(shape_mask, TILE, axis=0), TILE, axis=1)  24.6 us
  transfers between devices with their start and end apart: 2, of which 2 were waited for; matrix products, arithmetic and copies ran while one was open for 14% of the time, Pallas kernels for 0%

commit v1 on v0

--- a/solution.py
+++ b/solution.py
@@ -14,7 +14,12 @@
     int_mask = expand_shape(int_shape)
     amp_mask = expand_shape(amp_shape)
     whole_amp = lax.all_gather(amplitudes, "row", axis=0, tiled=True) * amp_mask
-    left = lax.all_gather(integrals, "col", axis=1, tiled=True) * int_mask
+    left = (
+        jnp.concatenate(
+            lax.all_to_all(jnp.stack([integrals] * lax.axis_size("col")), "col", 0, 0), axis=1
+        )
+        * int_mask
+    )
     total = jnp.dot(left, whole_amp, preferred_element_type=jnp.float32)
     return total.astype(jnp.bfloat16)
 

time: 411 us -> 537 us (1.31)
  waiting for transfers between devices: 314 us -> 439 us
  local copies, waits for them, and re-layouts: 55.8 us -> 32 us
  other arithmetic: 0.7 us -> 20.5 us
  starting transfers between devices: 0.04 us -> 8.62 us
    all_to_all x0 -> x1, waiting for transfers between devices: none -> 407 us  [per_device(): lax.all_to_all(jnp.stack([integrals] * lax.axis_size('col')), 'col', 0, 0)]
    all_gather x1 -> x0, waiting for transfers between devices: 157 us -> none  [per_device(): left = lax.all_gather(integrals, 'col', axis=1, tiled=True) * int_mask]
    all_gather x1, waiting for transfers between devices: 155 us -> 31.3 us  [per_device(): whole_amp = lax.all_gather(amplitudes, 'row', axis=0, tiled=True) * amp_mask]
    unnamed x4 -> x7, local copies, waits for them, and re-layouts: 30.7 us -> 9.97 us
    mul x0 -> x1, other arithmetic: none -> 20.4 us  [per_device(): jnp.concatenate(lax.all_to_all(jnp.stack([integrals] * lax.axis_size('col...]
    broadcast_in_dim x2 -> x1, local copies, waits for them, and re-layouts: 24.6 us -> 12.5 us  [expand_shape(): jnp.repeat(jnp.repeat(shape_mask, TILE, axis=0), TILE, axis=1)]
    another operation x0 -> x1, local copies, waits for them, and re-layouts: none -> 8.87 us  [per_device(): jnp.stack([integrals] * lax.axis_size('col'))]
    all_to_all x0 -> x1, starting transfers between devices: none -> 8.58 us  [per_device(): lax.all_to_all(jnp.stack([integrals] * lax.axis_size('col')), 'col', 0, 0)]
  transfers between devices with their start and end apart: 2 -> 2, of which waited for: 2 -> 2; matrix products, arithmetic and copies ran while one was open for 14% -> 8% of each run, Pallas kernels for 0% -> 0%
where the time goes in v1:
time: 537 us; the launch traced here: 536 us
  waiting for transfers between devices  439 us (82%)
  local copies, waits for them, and re-layouts  32 us (6%)
  matrix products  23 us (4%)
  other arithmetic  20.5 us (4%)
  between operations  13.5 us (3%)
  starting transfers between devices  8.62 us (2%)
    all_to_all x1, waiting for transfers between devices, per_device(): lax.all_to_all(jnp.stack([integrals] * lax.axis_size('col')), 'col', 0, 0)  407 us
    all_gather x1, waiting for transfers between devices, per_device(): whole_amp = lax.all_gather(amplitudes, 'row', axis=0, tiled=True) * amp_mask  31.3 us
    dot_general x1, matrix products, per_device(): total = jnp.dot(left, whole_amp, preferred_element_type=jnp.float32)  23 us
    mul x1, other arithmetic, per_device(): jnp.concatenate(lax.all_to_all(jnp.stack([integrals] * lax.axis_size('col...  20.4 us
    broadcast_in_dim x1, local copies, waits for them, and re-layouts, expand_shape(): jnp.repeat(jnp.repeat(shape_mask, TILE, axis=0), TILE, axis=1)  12.5 us
  transfers between devices with their start and end apart: 2, of which 2 were waited for; matrix products, arithmetic and copies ran while one was open for 8% of the time, Pallas kernels for 0%

profile of v1, /device:TPU:1, one launch (start us, length us, event | category | flops | bytes accessed | tf_op | source)
XLA Modules:
  0.0 536.4 jit_solution(15325847779379082286)
XLA Ops:
  6.5 2.7 copy.9
  9.2 8.9 %stack.2 = bf16[16,1280,640]{1,2,0:T(8,128)(2,1)} broadcast(bf16[1280,640]{0,1:T(8,128)(2,1)S(1)} %copy.9), dimensions={1,2} | broadcast | bytes 27852800 | tf_op jit(solution)/shard_map/stack | solution.py:19
  18.1 0.0 copy-start
  18.1 0.0 copy-start.1
  18.1 8.6 %all-to-all-start = ((bf16[16,1280,640]{1,2,0:T(8,128)(2,1)}), bf16[16,1280,640]{1,2,0:T(8,128)(2,1)}, u32[]{:S(2)}, u32[]{:S(2)}) async-start(bf16[16,1280,640]{1,2,0:T(8,128)(2,1)} %stack.2), calls=%async_computation | async-start | bytes 52428800 | tf_op jit(solution)/shard_map/all_to_all | solution.py:19
  26.7 0.0 all-gather.2.cloned.1.call-start
  26.7 0.7 all-gather.2.cloned.1.call-update
  27.4 0.0 copy-done
  27.4 0.1 copy.10
  27.5 0.1 broadcast_in_dim.12
  27.7 0.0 copy-done.1
  27.7 0.1 copy.11
  27.8 0.3 broadcast_in_dim.14
  28.2 12.5 %broadcast_in_dim.15 = bf16[10240,2,256]{2,1,0:T(2,128)(2,1)S(1)} broadcast(bf16[10240,2]{1,0:T(8,128)(2,1)S(1)} %bitcast.16), dimensions={0,1} | broadcast | bytes 10526720 | tf_op jit(solution)/shard_map/broadcast_in_dim | solution.py:10
  40.7 7.2 %copy.13 = bf16[1280,8,2,256]{3,1,2,0:T(8,128)(2,1)} copy(bf16[1280,8,2,256]{3,2,1,0:T(2,128)(2,1)S(1)} %bitcast.14) | data formatting | bytes 20971520
  48.0 406.9 %all-to-all-done = bf16[16,1280,640]{1,2,0:T(8,128)(2,1)} async-done(((bf16[16,1280,640]{1,2,0:T(8,128)(2,1)}), bf16[16,1280,640]{1,2,0:T(8,128)(2,1)}, u32[]{:S(2)}, u32[]{:S(2)}) %all-to-all-start) | async-done | bytes 26214432 | tf_op jit(solution)/shard_map/all_to_all | solution.py:19
  454.8 20.4 %bitcast_multiply_fusion = bf16[1280,10240]{0,1:T(8,128)(2,1)} fusion(bf16[16,1280,640]{1,2,0:T(8,128)(2,1)} %all-to-all-done, bf16[1280,40]{0,1:T(8,128)(2,1)S(1)} %bitcast.18), kind=kLoop, calls=%fused_computation | loop fusion | flops 13107200 | bytes 52531200 | tf_op jit(solution)/shard_map/mul | solution.py:18
  475.3 31.3 %all-gather.2.cloned.1.call-done = bf16[10240,512]{1,0:T(8,128)(2,1)} async-done(((bf16[1280,512]{1,0:T(8,128)(2,1)}), bf16[10240,512]{1,0:T(8,128)(2,1)}) %all-gather.2.cloned.1.call-update) | async-done | bytes 10485776 | tf_op jit(solution)/shard_map/all_gather | solution.py:16
  506.5 23.0 %fusion.2 = bf16[1280,512]{1,0:T(8,128)(2,1)} fusion(bf16[1280,10240]{0,1:T(8,128)(2,1)} %bitcast_multiply_fusion, bf16[10240,512]{1,0:T(8,128)(2,1)} %all-gather.2.cloned.1.call-done, bf16[10240,512]{1,0:T(8,128)(2,1)} %bitcast.15), kind=kOutput, calls=%fused_computation.3 | convolution fusion | flops 13427671040 | bytes 48496640 | tf_op jit(solution)/shard_map/dot_general | solution.py:23
  (3 shorter events, 0.0 us)
Async XLA Ops:
  18.1 9.3 %copy-start = (s32[5,40]{1,0:T(8,128)S(1)}, s32[5,40]{1,0:T(8,128)}, u32[]{:S(2)}) copy-start(s32[5,40]{1,0:T(8,128)} %param.6) | copy-start | bytes 2404
  18.1 9.6 %copy-start.1 = (s32[40,2]{0,1:T(2,128)S(1)}, s32[40,2]{0,1:T(2,128)}, u32[]{:S(2)}) copy-start(s32[40,2]{0,1:T(2,128)} %param.7) | copy-start | bytes 964
  18.1 436.7 %all-to-all-start = ((bf16[16,1280,640]{1,2,0:T(8,128)(2,1)}), bf16[16,1280,640]{1,2,0:T(8,128)(2,1)}, u32[]{:S(2)}, u32[]{:S(2)}) async-start(bf16[16,1280,640]{1,2,0:T(8,128)(2,1)} %stack.2), calls=%async_computation | async-start | bytes 52428800 | tf_op jit(solution)/shard_map/all_to_all | solution.py:19
  26.7 479.8 %all-gather.2.cloned.1.call-start = ((), (), s32[]{:S(2)}) async-start(), calls=%async_computation.1 | async-start | bytes 11796480 | tf_op jit(solution)/shard_map/all_gather | solution.py:16
Sparse Core Ops, SparseCore 0:
  29.2 477.3 all-gather.1
